TPU v7x, 32 devices: a whole 2x2x4 slice. The times are simulated.
32 devices in a mesh: rows: 8 (over z, y), grp: 4 (over x, core).
Axes of the slice: x: 2, y: 2, z: 4, core: 2. Of those that a mesh axis runs over, the one named last changes fastest.
Arguments:
- panel: float32 [8192, 256], P(('rows', 'grp')), may hold values from -6000 to 6000
- trailing: float32 [8192, 2048], P(('rows', 'grp')), may hold values from -6000 to 6000
Outputs:
- upper_panel: float32 [256, 256], replicated
- projection: float32 [256, 2048], replicated
- updated: float32 [8192, 2048], P(('rows', 'grp'))
- upper_next: float32 [256, 256], replicated
All inputs are finite; a program needn't handle non-finite values.
Results may differ from a plain program's by a relative error of at most 0.00019.
Values sent between devices are 32-bit elements; how exact they have to be, the bound alone decides.
A program may use at most 128 MiB of HBM per device.

v0:
```python
import jax
import jax.numpy as jnp
from jax import lax
from jax.sharding import PartitionSpec as P


def cross(left, right):
    return lax.dot_general(
        left,
        right,
        (((0,), (0,)), ((), ())),
        precision=lax.Precision.HIGHEST,
        preferred_element_type=jnp.float32,
    )


def product(left, right):
    return jnp.dot(left, right, precision=lax.Precision.HIGHEST, preferred_element_type=jnp.float32)


def lower_inverse(lower):
    order = lower.shape[0]
    result = jnp.zeros((order, order), jnp.float32)
    for index in range(order):
        unit = (jnp.arange(order) == index).astype(jnp.float32)
        new_row = (
            unit - jnp.dot(lower[index, :], result, precision=lax.Precision.HIGHEST)
        ) / lower[index, index]
        result = result.at[index, :].set(new_row)
    return result


def factor_pair(matrix):
    order = matrix.shape[0]
    if order <= 16 or order % 2 == 1:
        lower = jnp.zeros((order, order), jnp.float32)
        row_ids = jnp.arange(order)
        for index in range(order):
            column = matrix[:, index] - jnp.dot(
                lower, lower[index, :], precision=lax.Precision.HIGHEST
            )
            pivot = jnp.sqrt(column[index])
            lower = lower.at[:, index].set(jnp.where(row_ids >= index, column / pivot, 0.0))
        return (lower, lower_inverse(lower))
    middle = order // 2
    first_low, first_inv = factor_pair(matrix[:middle, :middle])
    below = product(matrix[middle:, :middle], first_inv.T)
    schur = matrix[middle:, middle:] - product(below, below.T)
    second_low, second_inv = factor_pair(schur)
    below_inv = -product(second_inv, product(below, first_inv))
    zeros_block = jnp.zeros((middle, order - middle), jnp.float32)
    lower = jnp.concatenate(
        [
            jnp.concatenate([first_low, zeros_block], axis=1),
            jnp.concatenate([below, second_low], axis=1),
        ],
        axis=0,
    )
    inverse = jnp.concatenate(
        [
            jnp.concatenate([first_inv, zeros_block], axis=1),
            jnp.concatenate([below_inv, second_inv], axis=1),
        ],
        axis=0,
    )
    return (lower, inverse)


def upper_of(matrix):
    return factor_pair(matrix)[0].T


def per_device(panel, trailing):
    inv_rows = 1.0 / (panel.shape[0] * lax.axis_size(("rows", "grp")))
    width = panel.shape[1]
    gram_panel, cross_terms, gram_head = lax.psum(
        (
            cross(panel, panel),
            cross(panel, trailing),
            cross(trailing[:, :width], trailing[:, :width]),
        ),
        ("rows", "grp"),
    )
    lower, lower_inv = factor_pair(gram_panel * inv_rows)
    upper_panel = lower.T
    inverse = lower_inv.T
    ortho_basis = product(panel, inverse)
    projection = cross(inverse, cross_terms) * inv_rows
    updated = trailing - product(ortho_basis, projection)
    head_proj = projection[:, :width]
    upper_next = upper_of(gram_head * inv_rows - cross(head_proj, head_proj))
    return (upper_panel, projection, updated, upper_next)


def solution(mesh):
    return jax.shard_map(
        per_device,
        mesh=mesh,
        in_specs=(P(("rows", "grp"), None), P(("rows", "grp"), None)),
        out_specs=(P(), P(), P(("rows", "grp"), None), P()),
        check_vma=False,
    )
```

profile of v0, /device:TPU:0, one launch (start us, length us, event | category | flops | bytes accessed | tf_op | source)
XLA Modules:
  0.0 1853.8 jit_solution(8966382655848866502)
XLA Ops:
  7.2 2.4 fusion.1984
  9.6 4.8 fusion.2984
  25.9 130.2 %all-reduce.122.cloned.1.call-done = (f32[256,256]{1,0:T(8,128)}, f32[256,2048]{1,0:T(8,128)}, f32[256,256]{1,0:T(8,128)}) async-done(((f32[256,256]{1,0:T(8,128)}, f32[256,2048]{1,0:T(8,128)}, f32[256,256]{1,0:T(8,128)}), (f32[256,256]{1,0:T(8,128)}, f32[256,2048]{1,0:T(8,128)}, f32[256,256]{1,0:T(8,128)})) %all-reduce.122.cloned.1.call-update) | async-done | bytes 2621456 | tf_op jit(solution)/shard_map/psum | solution.py:76
  198.2 1.5 fusion.985
  204.1 1.5 fusion.993
  207.0 1.5 fusion.997
  210.0 1.5 fusion.1001
  211.5 1.5 fusion.1003
  308.7 1.5 fusion.1051
  314.6 1.5 fusion.1059
  317.5 1.5 fusion.1063
  571.1 1.5 fusion.1215
  577.0 1.5 fusion.1223
  774.8 1.5 fusion.1335
  783.5 1.5 fusion.1347
  983.4 1.5 fusion.1463
  986.3 1.5 fusion.1467
  995.1 1.5 fusion.1479
  1003.9 1.9 convolution_multiply_fusion
  1196.8 1.5 fusion.1591
  1205.6 1.5 fusion.1603
  1214.4 1.5 fusion.1615
  1406.4 1.5 fusion.1719
  1415.2 1.5 fusion.1731
  1424.1 1.5 fusion.1743
  1615.9 1.5 fusion.1847
  1624.7 1.5 fusion.1859
  1633.6 1.5 fusion.1871
  1788.3 1.5 fusion.1951
  1789.8 1.5 fusion.1953
  1798.6 1.5 fusion.1965
  1840.4 4.9 convolution_subtract_fusion
  (4283 shorter events, 1312.7 us)
Async XLA Ops:
  7.2 2.5 copy-start
  7.2 148.9 %all-reduce.122.cloned.1.call-start = ((), (), s32[]{:S(2)}) async-start(), calls=%async_computation | async-start | bytes 5242880 | tf_op jit(solution)/shard_map/psum | solution.py:76
  157.6 1578.2 %copy-start.35 = (f32[16]{0:T(128)}, f32[16]{0:T(128)S(1)}, u32[]{:S(2)}) copy-start(f32[16]{0:T(128)S(1)} %get-tuple-element.13089) | copy-start | bytes 196
  192.9 2.3 copy-start.8
  325.1 52.1 %copy-start.24 = (f32[16,16]{1,0:T(8,128)}, f32[16,16]{1,0:T(8,128)S(1)}, u32[]{:S(2)}) copy-start(f32[16,16]{1,0:T(8,128)S(1)} %fusion.2173) | copy-start | bytes 3076
  561.5 2.3 copy-start.4
  734.8 59.3 %copy-start.26 = (f32[16,16]{1,0:T(8,128)}, f32[16,16]{1,0:T(8,128)S(1)}, u32[]{:S(2)}) copy-start(f32[16,16]{1,0:T(8,128)S(1)} %fusion.2165) | copy-start | bytes 3076
  893.9 110.0 %copy-start.20 = (f32[256,2048]{1,0:T(8,128)S(1)}, f32[256,2048]{1,0:T(8,128)}, u32[]{:S(2)}) copy-start(f32[256,2048]{1,0:T(8,128)} %get-tuple-element.12621) | copy-start | bytes 6291460
  943.6 62.3 %copy-start.22 = (f32[16,16]{1,0:T(8,128)}, f32[16,16]{1,0:T(8,128)S(1)}, u32[]{:S(2)}) copy-start(f32[16,16]{1,0:T(8,128)S(1)} %fusion.2161) | copy-start | bytes 3076
  1003.9 3.3 copy-start.21
  1156.9 59.4 %copy-start.28 = (f32[16,16]{1,0:T(8,128)}, f32[16,16]{1,0:T(8,128)S(1)}, u32[]{:S(2)}) copy-start(f32[16,16]{1,0:T(8,128)S(1)} %fusion.2157) | copy-start | bytes 3076
  1575.8 59.4 %copy-start.29 = (f32[16,16]{1,0:T(8,128)}, f32[16,16]{1,0:T(8,128)S(1)}, u32[]{:S(2)}) copy-start(f32[16,16]{1,0:T(8,128)S(1)} %fusion.2149) | copy-start | bytes 3076
  1612.2 2.3 copy-start.16
  1695.9 79.1 %copy-start.9 = (f32[16,16]{1,0:T(8,128)S(1)}, f32[16,16]{1,0:T(8,128)}, u32[]{:S(2)}) copy-start(f32[16,16]{1,0:T(8,128)} %copy-done.8) | copy-start | bytes 3076
  1752.9 84.1 %copy-start.15 = (f32[16,16]{1,0:T(8,128)S(1)}, f32[16,16]{1,0:T(8,128)}, u32[]{:S(2)}) copy-start(f32[16,16]{1,0:T(8,128)} %copy-done.14) | copy-start | bytes 3076
  1756.7 81.2 %copy-start.17 = (f32[16,16]{1,0:T(8,128)S(1)}, f32[16,16]{1,0:T(8,128)}, u32[]{:S(2)}) copy-start(f32[16,16]{1,0:T(8,128)} %copy-done.16) | copy-start | bytes 3076
  1759.1 79.5 %copy-start.7 = (f32[16,16]{1,0:T(8,128)S(1)}, f32[16,16]{1,0:T(8,128)}, u32[]{:S(2)}) copy-start(f32[16,16]{1,0:T(8,128)} %copy-done.6) | copy-start | bytes 3076
  1772.5 29.9 %copy-start.36 = (f32[16]{0:T(128)S(1)}, f32[16]{0:T(128)}, u32[]{:S(2)}) copy-start(f32[16]{0:T(128)} %copy-done.35) | copy-start | bytes 196
  1773.8 64.8 %copy-start.30 = (f32[32,32]{1,0:T(8,128)S(1)}, f32[32,32]{1,0:T(8,128)}, u32[]{:S(2)}) copy-start(f32[32,32]{1,0:T(8,128)} %select_maximum_fusion.23) | copy-start | bytes 12292
  1774.6 65.8 %copy-start.18 = (f32[256,2048]{1,0:T(8,128)S(1)}, f32[256,2048]{1,0:T(8,128)}, u32[]{:S(2)}) copy-start(f32[256,2048]{1,0:T(8,128)} %param.2019) | copy-start | bytes 6291460
  1775.0 62.8 %copy-start.34 = (f32[32,32]{1,0:T(8,128)S(1)}, f32[32,32]{1,0:T(8,128)}, u32[]{:S(2)}) copy-start(f32[32,32]{1,0:T(8,128)} %select_maximum_fusion.21) | copy-start | bytes 12292
  1776.6 62.2 %copy-start.31 = (f32[32,32]{1,0:T(8,128)S(1)}, f32[32,32]{1,0:T(8,128)}, u32[]{:S(2)}) copy-start(f32[32,32]{1,0:T(8,128)} %select_maximum_fusion.19) | copy-start | bytes 12292
  1778.8 2.3 copy-start.3
  1840.3 4.9 copy-start.11
  1840.3 4.9 copy-start.25
  1840.4 4.9 copy-start.32
  1840.4 5.0 copy-start.13
  1840.4 5.0 copy-start.27
  1840.4 5.0 copy-start.33
  1840.4 5.1 copy-start.5
  1840.4 5.2 copy-start.2
  1840.4 5.2 copy-start.23
  (6 other events, 12.5 us)
Sparse Core Ops, SparseCore 0:
  15.8 140.1 all-reduce.121
where the time goes:
time: 1880 us; the launch traced here: 1850 us
  matrix products  562 us (30%)
  local copies, waits for them, and re-layouts  450 us (24%)
  between operations  356 us (19%)
  other arithmetic  355 us (19%)
  waiting for transfers between devices  130 us (7%)
    dot_general x496, matrix products, lower_inverse(): jnp.dot(lower[index, :], result, precision=lax.Precision.HIGHEST)  465 us
    another operation x943, other arithmetic  345 us
    slice x480, local copies, waits for them, and re-layouts, factor_pair(): pivot = jnp.sqrt(column[index])  288 us
    psum x1, waiting for transfers between devices, per_device(): lax.psum((cross(panel, panel), cross(panel, trailing), cross(trailing[:,...  130 us
    dot_general x481, matrix products, factor_pair(): jnp.dot(lower, lower[index, :], precision=lax.Precision.HIGHEST)  63.9 us
    scatter x512, local copies, waits for them, and re-layouts, factor_pair(): lower.at[:, index].set(jnp.where(row_ids >= index, column / pivot, 0.0))  43.8 us
    another operation x512, local copies, waits for them, and re-layouts  43.5 us
    slice x62, local copies, waits for them, and re-layouts, lower_inverse(): lower[index, index]  41.8 us

commit v1 on v0

--- a/solution.py
+++ b/solution.py
@@ -71,15 +71,20 @@
 
 
 def per_device(panel, trailing):
+
+    def replace_array_here(raw):
+        for b in ("grp", "rows"):
+            raw = lax.psum(raw, axis_name=b)
+        return raw
+
     inv_rows = 1.0 / (panel.shape[0] * lax.axis_size(("rows", "grp")))
     width = panel.shape[1]
-    gram_panel, cross_terms, gram_head = lax.psum(
+    gram_panel, cross_terms, gram_head = replace_array_here(
         (
             cross(panel, panel),
             cross(panel, trailing),
             cross(trailing[:, :width], trailing[:, :width]),
-        ),
-        ("rows", "grp"),
+        )
     )
     lower, lower_inv = factor_pair(gram_panel * inv_rows)
     upper_panel = lower.T

time: 1880 us -> 1930 us (1.027)
  waiting for transfers between devices: 130 us -> 173 us
    psum x1 -> x2, waiting for transfers between devices: 130 us -> 173 us  [replace_array_here(): raw = lax.psum(raw, axis_name=b)]
where the time goes in v1:
time: 1930 us; the launch traced here: 1900 us
  matrix products  568 us (29%)
  local copies, waits for them, and re-layouts  453 us (23%)
  between operations  357 us (18%)
  other arithmetic  354 us (18%)
  waiting for transfers between devices  173 us (9%)
    dot_general x496, matrix products, lower_inverse(): jnp.dot(lower[index, :], result, precision=lax.Precision.HIGHEST)  471 us
    another operation x943, other arithmetic  345 us
    slice x480, local copies, waits for them, and re-layouts, factor_pair(): pivot = jnp.sqrt(column[index])  289 us
    psum x2, waiting for transfers between devices, replace_array_here(): raw = lax.psum(raw, axis_name=b)  173 us
    dot_general x481, matrix products, factor_pair(): jnp.dot(lower, lower[index, :], precision=lax.Precision.HIGHEST)  63.9 us
    scatter x512, local copies, waits for them, and re-layouts, factor_pair(): lower.at[:, index].set(jnp.where(row_ids >= index, column / pivot, 0.0))  43.8 us
    slice x62, local copies, waits for them, and re-layouts, lower_inverse(): lower[index, index]  43.6 us
    another operation x512, local copies, waits for them, and re-layouts  43.4 us

profile of v1, /device:TPU:0, one launch (start us, length us, event | category | flops | bytes accessed | tf_op | source)
XLA Modules:
  0.0 1904.9 jit_solution(5672085761019120734)
XLA Ops:
  7.2 2.4 fusion.1984
  9.6 4.8 fusion.2984
  15.8 62.8 %all-reduce.126.cloned.1.call-done = (f32[256,256]{1,0:T(8,128)}, f32[256,2048]{1,0:T(8,128)}, f32[256,256]{1,0:T(8,128)}) async-done(((f32[256,256]{1,0:T(8,128)}, f32[256,2048]{1,0:T(8,128)}, f32[256,256]{1,0:T(8,128)}), (f32[256,256]{1,0:T(8,128)}, f32[256,2048]{1,0:T(8,128)}, f32[256,256]{1,0:T(8,128)})) %all-reduce.126.cloned.1.call-update) | async-done | bytes 2621456 | tf_op jit(solution)/shard_map/psum | solution.py:77
  88.7 110.1 %all-reduce.124.cloned.1.call-done = (f32[256,256]{1,0:T(8,128)}, f32[256,2048]{1,0:T(8,128)}, f32[256,256]{1,0:T(8,128)}) async-done(((f32[256,256]{1,0:T(8,128)}, f32[256,2048]{1,0:T(8,128)}, f32[256,256]{1,0:T(8,128)}), (f32[256,256]{1,0:T(8,128)}, f32[256,2048]{1,0:T(8,128)}, f32[256,256]{1,0:T(8,128)})) %all-reduce.124.cloned.1.call-update) | async-done | bytes 2621456 | tf_op jit(solution)/shard_map/psum | solution.py:77
  241.0 1.5 fusion.985
  244.0 1.5 fusion.989
  245.5 1.5 fusion.991
  257.4 1.5 fusion.1007
  350.8 1.5 fusion.1049
  353.7 1.5 fusion.1053
  355.3 1.5 fusion.1055
  367.2 1.5 fusion.1071
  614.0 1.5 fusion.1213
  627.4 1.5 fusion.1231
  824.9 1.5 fusion.1341
  838.3 1.5 fusion.1359
  1034.9 1.5 fusion.1469
  1036.5 1.5 fusion.1471
  1048.3 1.5 fusion.1487
  1051.1 1.9 convolution_multiply_fusion
  1246.1 1.5 fusion.1593
  1255.0 1.5 fusion.1605
  1262.4 1.5 fusion.1615
  1456.3 1.5 fusion.1721
  1465.3 1.5 fusion.1733
  1472.7 1.5 fusion.1743
  1666.5 1.5 fusion.1849
  1675.5 1.5 fusion.1861
  1682.9 1.5 fusion.1871
  1840.7 1.5 fusion.1955
  1849.6 1.5 fusion.1967
  1891.6 4.9 convolution_subtract_fusion
  (4286 shorter events, 1321.7 us)
Async XLA Ops:
  7.2 2.5 copy-start
  7.2 71.4 %all-reduce.126.cloned.1.call-start = ((), (), s32[]{:S(2)}) async-start(), calls=%async_computation.1 | async-start | bytes 5242880 | tf_op jit(solution)/shard_map/psum | solution.py:77
  15.7 183.1 %all-reduce.124.cloned.1.call-start = ((), (), s32[]{:S(2)}) async-start(), calls=%async_computation | async-start | bytes 5242880 | tf_op jit(solution)/shard_map/psum | solution.py:77
  200.4 1585.1 %copy-start.35 = (f32[16]{0:T(128)}, f32[16]{0:T(128)S(1)}, u32[]{:S(2)}) copy-start(f32[16]{0:T(128)S(1)} %get-tuple-element.13092) | copy-start | bytes 196
  235.8 2.3 copy-start.8
  345.6 2.3 copy-start.10
  368.8 52.3 %copy-start.24 = (f32[16,16]{1,0:T(8,128)}, f32[16,16]{1,0:T(8,128)S(1)}, u32[]{:S(2)}) copy-start(f32[16,16]{1,0:T(8,128)S(1)} %fusion.2173) | copy-start | bytes 3076
  780.4 59.8 %copy-start.26 = (f32[16,16]{1,0:T(8,128)}, f32[16,16]{1,0:T(8,128)S(1)}, u32[]{:S(2)}) copy-start(f32[16,16]{1,0:T(8,128)S(1)} %fusion.2165) | copy-start | bytes 3076
  816.7 2.3 copy-start.12
  940.5 110.6 %copy-start.20 = (f32[256,2048]{1,0:T(8,128)S(1)}, f32[256,2048]{1,0:T(8,128)}, u32[]{:S(2)}) copy-start(f32[256,2048]{1,0:T(8,128)} %get-tuple-element.12621) | copy-start | bytes 6291460
  990.6 62.5 %copy-start.22 = (f32[16,16]{1,0:T(8,128)}, f32[16,16]{1,0:T(8,128)S(1)}, u32[]{:S(2)}) copy-start(f32[16,16]{1,0:T(8,128)S(1)} %fusion.2161) | copy-start | bytes 3076
  1051.1 3.3 copy-start.21
  1204.8 59.5 %copy-start.28 = (f32[16,16]{1,0:T(8,128)}, f32[16,16]{1,0:T(8,128)S(1)}, u32[]{:S(2)}) copy-start(f32[16,16]{1,0:T(8,128)S(1)} %fusion.2157) | copy-start | bytes 3076
  1625.0 59.6 %copy-start.29 = (f32[16,16]{1,0:T(8,128)}, f32[16,16]{1,0:T(8,128)S(1)}, u32[]{:S(2)}) copy-start(f32[16,16]{1,0:T(8,128)S(1)} %fusion.2149) | copy-start | bytes 3076
  1745.5 79.1 %copy-start.9 = (f32[16,16]{1,0:T(8,128)S(1)}, f32[16,16]{1,0:T(8,128)}, u32[]{:S(2)}) copy-start(f32[16,16]{1,0:T(8,128)} %copy-done.8) | copy-start | bytes 3076
  1802.7 85.5 %copy-start.15 = (f32[16,16]{1,0:T(8,128)S(1)}, f32[16,16]{1,0:T(8,128)}, u32[]{:S(2)}) copy-start(f32[16,16]{1,0:T(8,128)} %copy-done.14) | copy-start | bytes 3076
  1806.4 82.6 %copy-start.17 = (f32[16,16]{1,0:T(8,128)S(1)}, f32[16,16]{1,0:T(8,128)}, u32[]{:S(2)}) copy-start(f32[16,16]{1,0:T(8,128)} %copy-done.16) | copy-start | bytes 3076
  1808.8 81.0 %copy-start.7 = (f32[16,16]{1,0:T(8,128)S(1)}, f32[16,16]{1,0:T(8,128)}, u32[]{:S(2)}) copy-start(f32[16,16]{1,0:T(8,128)} %copy-done.6) | copy-start | bytes 3076
  1822.0 29.9 %copy-start.36 = (f32[16]{0:T(128)S(1)}, f32[16]{0:T(128)}, u32[]{:S(2)}) copy-start(f32[16]{0:T(128)} %copy-done.35) | copy-start | bytes 196
  1823.4 66.4 %copy-start.30 = (f32[32,32]{1,0:T(8,128)S(1)}, f32[32,32]{1,0:T(8,128)}, u32[]{:S(2)}) copy-start(f32[32,32]{1,0:T(8,128)} %select_maximum_fusion.23) | copy-start | bytes 12292
  1824.1 67.4 %copy-start.18 = (f32[256,2048]{1,0:T(8,128)S(1)}, f32[256,2048]{1,0:T(8,128)}, u32[]{:S(2)}) copy-start(f32[256,2048]{1,0:T(8,128)} %param.2019) | copy-start | bytes 6291460
  1824.6 64.4 %copy-start.34 = (f32[32,32]{1,0:T(8,128)S(1)}, f32[32,32]{1,0:T(8,128)}, u32[]{:S(2)}) copy-start(f32[32,32]{1,0:T(8,128)} %select_maximum_fusion.21) | copy-start | bytes 12292
  1826.1 63.8 %copy-start.31 = (f32[32,32]{1,0:T(8,128)S(1)}, f32[32,32]{1,0:T(8,128)}, u32[]{:S(2)}) copy-start(f32[32,32]{1,0:T(8,128)} %select_maximum_fusion.19) | copy-start | bytes 12292
  1891.5 4.9 copy-start.11
  1891.5 4.9 copy-start.25
  1891.5 4.9 copy-start.32
  1891.5 5.0 copy-start.13
  1891.5 5.0 copy-start.27
  1891.5 5.0 copy-start.33
  1891.5 5.1 copy-start.5
  1891.6 5.2 copy-start.2
  1891.6 5.2 copy-start.23
  (7 other events, 14.9 us)
Sparse Core Ops, SparseCore 0:
  15.9 62.6 all-reduce.125
  82.5 116.2 all-reduce.123
